TPU v7x, 256 devices: a whole 4x4x8 slice. The times are simulated.
256 devices in a mesh: copy: 4 (over x_hi, core), space: 64 (over y, z, x_lo).
Axes of the slice: x: 4 (x_hi: 2, x_lo: 2; x = x_hi * 2 + x_lo), y: 4, z: 8, core: 2. Of those that a mesh axis runs over, the one named last changes fastest.
Arguments:
- noisy_tokens: bfloat16 [4, 256, 256, 384], P('copy', 'space'), may hold values from -6 to 6
- grad_out: bfloat16 [4, 256, 256, 384], P('copy', 'space'), may hold values from -6 to 6
- filter_weight: bfloat16 [2, 256, 256, 384], P(None, None, 'space'), may hold values from -4 to 4
- weight_in: bfloat16 [384, 1536], replicated, may hold values from -0.3125 to 0.3125
- weight_out: bfloat16 [1536, 384], replicated, may hold values from -0.15625 to 0.15625
- gain_one: float32 [384], replicated, may hold values from 0.1 to 1.9
- gain_two: float32 [384], replicated, may hold values from 0.1 to 1.9
Outputs:
- block_out: bfloat16 [4, 256, 256, 384], P('copy', 'space')
- grad_tokens: bfloat16 [4, 256, 256, 384], P('copy', 'space')
- grad_filter: float32 [2, 256, 256, 384], P(None, None, 'space')
- grad_weight_in: bfloat16 [384, 1536], replicated
- grad_weight_out: bfloat16 [1536, 384], replicated
- grad_gain_one: float32 [384], replicated
- grad_gain_two: float32 [384], replicated
All inputs are finite; a program needn't handle non-finite values.
Results may differ from a plain program's by a relative error of at most 0.024.
Values may be sent and summed in bfloat16 or wider, within the bound.
A program may use at most 128 MiB of HBM per device.

v0:
```python
import math
import jax
import jax.numpy as jnp
from jax import lax
from jax.sharding import PartitionSpec as P

EPS = 1e-06


def dft_parts(length):
    index = jnp.arange(length, dtype=jnp.int32)
    phase = index[:, None] * index[None, :] % length
    angle = phase.astype(jnp.float32) * (2.0 * math.pi / length)
    factor = 1.0 / math.sqrt(length)
    return (
        (jnp.cos(angle) * factor).astype(jnp.bfloat16),
        (jnp.sin(angle) * factor).astype(jnp.bfloat16),
    )


def row_table(length):
    cosine, sine = dft_parts(length)
    return jnp.stack([cosine, -sine])


def column_table(length, direction):
    cosine, sine = dft_parts(length)
    upper = jnp.stack([cosine, direction * sine], axis=1)
    lower = jnp.stack([-direction * sine, cosine], axis=1)
    return jnp.stack([upper, lower])


def layer_norm(values):
    centre = jnp.mean(values, axis=-1, keepdims=True)
    centred = values - centre
    variance = jnp.mean(centred * centred, axis=-1, keepdims=True)
    rstd_value = lax.rsqrt(variance + EPS)
    return (centred * rstd_value, rstd_value)


def norm_backward(upstream, normed, rstd_value, gain):
    scaled = upstream * gain
    result = (
        scaled
        - jnp.mean(scaled, axis=-1, keepdims=True)
        - normed * jnp.mean(scaled * normed, axis=-1, keepdims=True)
    ) * rstd_value
    lead = tuple(range(upstream.ndim - 1))
    return (result, jnp.sum(upstream * normed, axis=lead))


def apply_filter(spectrum, filter_weight, direction):
    real_part = spectrum[0].astype(jnp.float32)
    imag_part = spectrum[1].astype(jnp.float32)
    kernel_real = filter_weight[0].astype(jnp.float32)
    kernel_imag = direction * filter_weight[1].astype(jnp.float32)
    return jnp.stack(
        [
            kernel_real * real_part - kernel_imag * imag_part,
            kernel_real * imag_part + kernel_imag * real_part,
        ]
    )


def exact_gelu(values):
    return jax.nn.gelu(values, approximate=False)


def spectral(values, filter_weight, direction):
    width = values.shape[2]
    rows_tab = row_table(width)
    rows = jnp.einsum(
        "pkw,bhwc->pbhkc", rows_tab, values, preferred_element_type=jnp.float32
    ).astype(jnp.bfloat16)
    columns = lax.all_to_all(rows, "space", split_axis=3, concat_axis=2, tiled=True)
    height = columns.shape[2]
    spectrum = jnp.einsum(
        "qmph,pbhkc->qbmkc", column_table(height, 1), columns, preferred_element_type=jnp.float32
    ).astype(jnp.bfloat16)
    weighted = apply_filter(spectrum, filter_weight[:, None], direction).astype(jnp.bfloat16)
    returned = jnp.einsum(
        "qmph,pbhkc->qbmkc", column_table(height, -1), weighted, preferred_element_type=jnp.float32
    ).astype(jnp.bfloat16)
    back_rows = lax.all_to_all(returned, "space", split_axis=2, concat_axis=3, tiled=True)
    output = jnp.einsum("pkw,pbhkc->bhwc", rows_tab, back_rows, preferred_element_type=jnp.float32)
    return (output, spectrum)


def body(noisy_tokens, grad_out, filter_weight, weight_in, weight_out, gain_one, gain_two):
    batch, rows_dev, width, chans = noisy_tokens.shape
    inputs = noisy_tokens.astype(jnp.float32)
    normed_one, rstd_one = layer_norm(inputs)
    mixed_in = (normed_one * gain_one).astype(jnp.bfloat16)
    spatial, spectrum = spectral(mixed_in, filter_weight, 1)
    normed_two, rstd_two = layer_norm(spatial)
    mlp_in = (normed_two * gain_two).astype(jnp.bfloat16).reshape(-1, chans)
    preact = jnp.dot(mlp_in, weight_in, preferred_element_type=jnp.float32)
    activated = exact_gelu(preact).astype(jnp.bfloat16)
    mlp_out = jnp.dot(activated, weight_out, preferred_element_type=jnp.float32)
    block_out = (inputs + mlp_out.reshape(inputs.shape)).astype(jnp.bfloat16)
    upstream = grad_out.reshape(-1, chans)
    grad_act = jnp.dot(upstream, weight_out.T, preferred_element_type=jnp.float32)
    grad_pre = jax.vjp(exact_gelu, preact)[1](grad_act)[0].astype(jnp.bfloat16)
    sum_out = jnp.dot(activated.T, upstream, preferred_element_type=jnp.float32)
    sum_in = jnp.dot(mlp_in.T, grad_pre, preferred_element_type=jnp.float32)
    grad_mlp = jnp.dot(grad_pre, weight_in.T, preferred_element_type=jnp.float32).reshape(
        inputs.shape
    )
    grad_spatial, sum_gain_two = norm_backward(grad_mlp, normed_two, rstd_two, gain_two)
    back_spatial, adjoint = spectral(grad_spatial.astype(jnp.bfloat16), filter_weight, -1)
    spec_f = spectrum.astype(jnp.float32)
    adj_f = adjoint.astype(jnp.float32)
    filter_terms = jnp.stack(
        [
            jnp.sum(adj_f[0] * spec_f[0] + adj_f[1] * spec_f[1], axis=0),
            jnp.sum(adj_f[1] * spec_f[0] - adj_f[0] * spec_f[1], axis=0),
        ]
    )
    grad_filter = lax.psum(filter_terms.astype(jnp.bfloat16), "copy").astype(jnp.float32)
    grad_normed, sum_gain_one = norm_backward(back_spatial, normed_one, rstd_one, gain_one)
    grad_tokens = (grad_out.astype(jnp.float32) + grad_normed).astype(jnp.bfloat16)
    local_sums = (sum_in, sum_out, sum_gain_one, sum_gain_two)
    summed = lax.psum(
        (local_sums[0], local_sums[1], local_sums[2], local_sums[3]), ("copy", "space")
    )
    total_tokens = batch * lax.axis_size("copy") * rows_dev * lax.axis_size("space") * width
    factor = 1.0 / math.sqrt(total_tokens)
    return (
        block_out,
        grad_tokens,
        grad_filter,
        (summed[0] * factor).astype(jnp.bfloat16),
        (summed[1] * factor).astype(jnp.bfloat16),
        summed[2] * factor,
        summed[3] * factor,
    )


def solution(mesh):
    return jax.shard_map(
        body,
        mesh=mesh,
        in_specs=(
            P("copy", "space", None, None),
            P("copy", "space", None, None),
            P(None, None, "space", None),
            P(),
            P(),
            P(),
            P(),
        ),
        out_specs=(
            P("copy", "space", None, None),
            P("copy", "space", None, None),
            P(None, None, "space", None),
            P(),
            P(),
            P(),
            P(),
        ),
        check_vma=False,
    )
```

profile of v0, /device:TPU:1, one launch (start us, length us, event | category | flops | bytes accessed | tf_op | source)
XLA Modules:
  0.0 629.1 jit_solution(3767009619410764740)
XLA Ops:
  7.2 1.6 fusion.87
  8.8 1.6 multiply_convert_fusion.8
  10.5 1.4 copy.67
  13.5 3.0 copy.69
  16.5 13.8 %all-to-all-start = ((bf16[2,1,4,256,384]{4,0,2,1,3:T(2,128)(2,1)}), bf16[2,1,4,256,384]{4,0,2,1,3:T(2,128)(2,1)}, u32[]{:S(2)}, u32[]{:S(2)}) async-start(bf16[2,1,4,256,384]{4,0,2,1,3:T(2,128)(2,1)} %copy.69), calls=%async_computation | async-start | bytes 3145728 | tf_op jit(solution)/shard_map/all_to_all | solution.py:75
  30.3 2.8 fusion.94
  33.8 1.8 copy.126
  36.6 1.1 multiply_convert_fusion.5
  38.8 29.9 %all-to-all-done = bf16[2,1,4,256,384]{4,0,2,1,3:T(2,128)(2,1)} async-done(((bf16[2,1,4,256,384]{4,0,2,1,3:T(2,128)(2,1)}), bf16[2,1,4,256,384]{4,0,2,1,3:T(2,128)(2,1)}, u32[]{:S(2)}, u32[]{:S(2)}) %all-to-all-start) | async-done | bytes 1572896 | tf_op jit(solution)/shard_map/all_to_all | solution.py:75
  68.6 2.0 copy.70
  71.7 2.7 fusion.95
  75.4 2.2 fusion.44
  77.6 4.3 copy.77
  81.9 45.2 %all_to_all.60 = bf16[2,1,256,4,384]{4,0,3,1,2:T(2,128)(2,1)S(1)} all-to-all(bf16[2,1,256,4,384]{4,0,3,1,2:T(2,128)(2,1)S(1)} %copy.77), channel_id=1, replica_groups=mesh['copy'=4,'space'=64] {'space'}, dimensions={2} | all-to-all | bytes 3145728 | tf_op jit(solution)/shard_map/all_to_all | solution.py:84
  128.3 1.4 reshape.561
  129.7 2.3 bitcast_reduce_fusion
  133.1 15.5 %multiply_convert_fusion = (bf16[1024,1536]{1,0:T(8,128)(2,1)}, f32[1024,1536]{1,0:T(8,128)S(1)}, f32[1024,1536]{1,0:T(8,128)S(1)}) fusion(bf16[1024,384]{1,0:T(8,128)(2,1)S(1)} %bitcast.255, bf16[384,1536]{1,0:T(8,128)(2,1)S(1)} %copy-done), kind=kOutput, calls=%fused_computation.3 | convolution fusion | flops 1310195712 | bytes 17694720 | tf_op jit(solution)/shard_map/dot_general | solution.py:97
  148.6 3.3 add_convert_fusion
  151.9 1.9 multiply_reduce_fusion.2
  153.8 1.1 multiply_reduce_fusion
  156.1 1.3 div.31
  157.4 4.0 fusion.40
  161.3 4.9 copy.84
  166.2 7.7 %all-to-all-start.2 = ((bf16[2,1,4,256,384]{4,0,2,1,3:T(2,128)(2,1)}), bf16[2,1,4,256,384]{4,0,2,1,3:T(2,128)(2,1)S(1)}, u32[]{:S(2)}, u32[]{:S(2)}) async-start(bf16[2,1,4,256,384]{4,0,2,1,3:T(2,128)(2,1)} %copy.84), calls=%async_computation.2 | async-start | bytes 3145728 | tf_op jit(solution)/shard_map/all_to_all | solution.py:75
  174.2 5.2 fusion.98
  179.3 3.2 fusion.99
  182.6 31.1 %all-to-all-done.2 = bf16[2,1,4,256,384]{4,0,2,1,3:T(2,128)(2,1)S(1)} async-done(((bf16[2,1,4,256,384]{4,0,2,1,3:T(2,128)(2,1)}), bf16[2,1,4,256,384]{4,0,2,1,3:T(2,128)(2,1)S(1)}, u32[]{:S(2)}, u32[]{:S(2)}) %all-to-all-start.2) | async-done | bytes 1572896 | tf_op jit(solution)/shard_map/all_to_all | solution.py:75
  214.9 2.6 copy.87
  217.5 4.3 fusion.96
  223.9 3.1 copy.90
  227.0 8.3 %all-to-all-start.3 = ((bf16[2,1,256,4,384]{4,0,3,1,2:T(2,128)(2,1)}), bf16[2,1,256,4,384]{4,0,3,1,2:T(2,128)(2,1)S(1)}, u32[]{:S(2)}, u32[]{:S(2)}) async-start(bf16[2,1,256,4,384]{4,0,3,1,2:T(2,128)(2,1)} %copy.90), calls=%async_computation.3 | async-start | bytes 3145728 | tf_op jit(solution)/shard_map/all_to_all | solution.py:84
  235.6 3.4 fusion.57
  241.0 1.3 pad_maximum_fusion
  242.4 2.3 copy.82
  244.7 5.1 fusion.97
  249.8 3.1 copy.81
  252.9 215.0 %all-reduce.7.cloned.1.call-done = (f32[384,1536]{1,0:T(8,128)}, f32[1536,384]{1,0:T(8,128)}) async-done(((f32[384,1536]{1,0:T(8,128)}, f32[1536,384]{1,0:T(8,128)}), (f32[384,1536]{1,0:T(8,128)}, f32[1536,384]{1,0:T(8,128)})) %all-reduce.7.cloned.1.call-update) | async-done | bytes 4718608 | tf_op jit(solution)/shard_map/psum | solution.py:123
  467.9 3.0 multiply_convert_fusion.1
  470.9 1.2 multiply_convert_fusion.2
  472.0 55.6 %all-reduce.5.cloned.1.call-done = bf16[2,256,4,384]{1,3,2,0:T(8,128)(2,1)} async-done(((bf16[2,256,4,384]{1,3,2,0:T(8,128)(2,1)}), bf16[2,256,4,384]{1,3,2,0:T(8,128)(2,1)}) %all-reduce.5.cloned.1.call-update) | async-done | bytes 1572880 | tf_op jit(solution)/shard_map/psum | solution.py:119
  527.7 3.9 copy.100
  533.1 2.6 fusion.18
  535.7 76.1 %all-reduce = (f32[384]{0:T(512)}, f32[384]{0:T(512)}) all-reduce(f32[384]{0:T(512)} %get-tuple-element.28, f32[384]{0:T(512)S(1)} %copy-done.27), channel_id=1, replica_groups=mesh['copy'=4,'space'=64] {'copy','space'}, use_global_device_ids=true, to_apply=%region_12.13 | all-reduce | flops 768 | bytes 6144 | tf_op jit(solution)/shard_map/psum | solution.py:123
  611.8 1.3 broadcast_multiply_fusion.7
  613.1 1.3 broadcast_multiply_fusion.8
  615.1 3.4 fusion.17
  618.5 2.4 copy.98
  620.9 1.2 copy.99
  (98 shorter events, 17.7 us)
Async XLA Ops:
  7.2 125.9 %copy-start = (bf16[384,1536]{1,0:T(8,128)(2,1)S(1)}, bf16[384,1536]{1,0:T(8,128)(2,1)}, u32[]{:S(2)}) copy-start(bf16[384,1536]{1,0:T(8,128)(2,1)} %param.10) | copy-start | bytes 3538948
  10.5 1.8 copy-start.28
  11.9 0.9 copy-start.13
  11.9 1.0 copy-start.15
  12.8 3.7 copy-start.25
  16.5 52.1 %all-to-all-start = ((bf16[2,1,4,256,384]{4,0,2,1,3:T(2,128)(2,1)}), bf16[2,1,4,256,384]{4,0,2,1,3:T(2,128)(2,1)}, u32[]{:S(2)}, u32[]{:S(2)}) async-start(bf16[2,1,4,256,384]{4,0,2,1,3:T(2,128)(2,1)} %copy.69), calls=%async_computation | async-start | bytes 3145728 | tf_op jit(solution)/shard_map/all_to_all | solution.py:75
  33.8 40.6 %copy-start.4 = (bf16[1,256,4,384]{1,3,2,0:T(8,128)(2,1)}, bf16[1,256,4,384]{1,3,2,0:T(8,128)(2,1)S(1)}, u32[]{:S(2)}) copy-start(bf16[1,256,4,384]{1,3,2,0:T(8,128)(2,1)S(1)} %copy.124) | copy-start | bytes 2359300
  35.6 38.8 %copy-start.6 = (bf16[1,256,4,384]{1,3,2,0:T(8,128)(2,1)}, bf16[1,256,4,384]{1,3,2,0:T(8,128)(2,1)S(1)}, u32[]{:S(2)}) copy-start(bf16[1,256,4,384]{1,3,2,0:T(8,128)(2,1)S(1)} %copy.126) | copy-start | bytes 2359300
  70.6 1.0 copy-start.11
  70.6 1.0 copy-start.12
  74.4 1.0 copy-start.20
  74.4 1.0 copy-start.22
  132.0 0.7 copy-start.24
  133.0 15.5 %copy-start.19 = (bf16[1,4,256,384]{3,2,1,0:T(8,128)(2,1)}, bf16[1,4,256,384]{3,2,1,0:T(8,128)(2,1)S(1)}, u32[]{:S(2)}) copy-start(bf16[1,4,256,384]{3,2,1,0:T(8,128)(2,1)S(1)} %multiply_convert_fusion.4) | copy-start | bytes 2359300
  133.0 15.5 %copy-start.17 = (bf16[1,4,256,384]{3,2,1,0:T(8,128)(2,1)S(1)}, bf16[1,4,256,384]{3,2,1,0:T(8,128)(2,1)}, u32[]{:S(2)}) copy-start(bf16[1,4,256,384]{3,2,1,0:T(8,128)(2,1)} %param.8) | copy-start | bytes 2359300
  133.1 15.5 %copy-start.30 = (bf16[1536,384]{1,0:T(8,128)(2,1)S(1)}, bf16[1536,384]{1,0:T(8,128)(2,1)}, u32[]{:S(2)}) copy-start(bf16[1536,384]{1,0:T(8,128)(2,1)} %param.11) | copy-start | bytes 3538948
  151.8 1.9 copy-start.31
  153.8 1.2 copy-start.3
  166.2 47.4 %all-to-all-start.2 = ((bf16[2,1,4,256,384]{4,0,2,1,3:T(2,128)(2,1)}), bf16[2,1,4,256,384]{4,0,2,1,3:T(2,128)(2,1)S(1)}, u32[]{:S(2)}, u32[]{:S(2)}) async-start(bf16[2,1,4,256,384]{4,0,2,1,3:T(2,128)(2,1)} %copy.84), calls=%async_computation.2 | async-start | bytes 3145728 | tf_op jit(solution)/shard_map/all_to_all | solution.py:75
  173.9 293.9 %all-reduce.7.cloned.1.call-start = ((), (), s32[]{:S(2)}) async-start(), calls=%async_computation.5 | async-start | bytes 9437184 | tf_op jit(solution)/shard_map/psum | solution.py:123
  174.1 5.2 copy-start.18
  174.1 5.2 copy-start.32
  217.5 4.3 copy-start.5
  217.5 4.3 copy-start.7
  221.8 1.0 copy-start.21
  221.8 1.0 copy-start.23
  227.0 304.5 %all-to-all-start.3 = ((bf16[2,1,256,4,384]{4,0,3,1,2:T(2,128)(2,1)}), bf16[2,1,256,4,384]{4,0,3,1,2:T(2,128)(2,1)S(1)}, u32[]{:S(2)}, u32[]{:S(2)}) async-start(bf16[2,1,256,4,384]{4,0,3,1,2:T(2,128)(2,1)} %copy.90), calls=%async_computation.3 | async-start | bytes 3145728 | tf_op jit(solution)/shard_map/all_to_all | solution.py:84
  235.3 292.3 %all-reduce.5.cloned.1.call-start = ((), (), s32[]{:S(2)}) async-start(), calls=%async_computation.4 | async-start | bytes 3145728 | tf_op jit(solution)/shard_map/psum | solution.py:119
  235.6 3.9 copy-start.1
  235.6 4.8 copy-start.2
  467.8 3.0 copy-start.10
  532.1 0.9 copy-start.14
  532.2 1.0 copy-start.16
  532.2 1.0 copy-start.26
  532.2 0.9 copy-start.29
  533.1 2.6 copy-start.27
  533.1 81.9 %copy-start.8 = (f32[1,4,256,384]{2,3,1,0:T(8,128)S(1)}, f32[1,4,256,384]{2,3,1,0:T(8,128)}, u32[]{:S(2)}) copy-start(f32[1,4,256,384]{2,3,1,0:T(8,128)} %copy.81) | copy-start | bytes 4718596
  618.5 2.4 copy-start.9
Sparse Core Ops, SparseCore 0:
  182.7 285.0 all-reduce.6
  470.7 56.9 all-reduce.4
where the time goes:
time: 639 us; the launch traced here: 629 us
  waiting for transfers between devices  332 us (52%)
  blocking collectives  121 us (19%)
  matrix products  53.9 us (8%)
  local copies, waits for them, and re-layouts  50 us (8%)
  starting transfers between devices  30.3 us (5%)
  other arithmetic  27.3 us (4%)
  between operations  14.7 us (2%)
    psum x1, waiting for transfers between devices, body(): lax.psum((local_sums[0], local_sums[1], local_sums[2], local_sums[3]), ('...  215 us
    psum x1, blocking collectives, body(): lax.psum((local_sums[0], local_sums[1], local_sums[2], local_sums[3]), ('...  76.1 us
    all_to_all x2, waiting for transfers between devices, spectral(): lax.all_to_all(rows, 'space', split_axis=3, concat_axis=2, tiled=True)  61 us
    psum x1, waiting for transfers between devices, body(): lax.psum(filter_terms.astype(jnp.bfloat16), 'copy').astype(jnp.float32)  55.6 us
    all_to_all x1, blocking collectives, spectral(): lax.all_to_all(returned, 'space', split_axis=2, concat_axis=3, tiled=True)  45.2 us
    all_to_all x2, starting transfers between devices, spectral(): lax.all_to_all(rows, 'space', split_axis=3, concat_axis=2, tiled=True)  21.5 us
    unnamed x73, local copies, waits for them, and re-layouts  17.3 us
    dot_general x1, matrix products, body(): preact = jnp.dot(mlp_in, weight_in, preferred_element_type=jnp.float32)  15.5 us
  transfers between devices with their start and end apart: 5, of which 4 were waited for; matrix products, arithmetic and copies ran while one was open for 9% of the time, Pallas kernels for 0%

commit v1 on v0

--- a/solution.py
+++ b/solution.py
@@ -81,7 +81,12 @@
     returned = jnp.einsum(
         "qmph,pbhkc->qbmkc", column_table(height, -1), weighted, preferred_element_type=jnp.float32
     ).astype(jnp.bfloat16)
-    back_rows = lax.all_to_all(returned, "space", split_axis=2, concat_axis=3, tiled=True)
+    back_rows = jnp.concatenate(
+        lax.all_to_all(
+            jnp.stack(jnp.split(returned, lax.axis_size("space"), axis=2)), "space", 0, 0
+        ),
+        axis=3,
+    )
     output = jnp.einsum("pkw,pbhkc->bhwc", rows_tab, back_rows, preferred_element_type=jnp.float32)
     return (output, spectrum)
 

time: 639 us -> 623 us (0.975)
  waiting for transfers between devices: 332 us -> 292 us
  local copies, waits for them, and re-layouts: 50 us -> 78.1 us
    unnamed x73 -> x197, local copies, waits for them, and re-layouts: 17.3 us -> 57.1 us
    psum x1, waiting for transfers between devices: 215 us -> 176 us  [body(): lax.psum((local_sums[0], local_sums[1], local_sums[2], local_sums[3]), ('...]
    convert_element_type x2 -> x0, local copies, waits for them, and re-layouts: 7.42 us -> none  [spectral(): returned = jnp.einsum('qmph,pbhkc->qbmkc', column_table(height, -1), weig...]
  transfers between devices with their start and end apart: 5 -> 5, of which waited for: 4 -> 4; matrix products, arithmetic and copies ran while one was open for 9% -> 14% of each run, Pallas kernels for 0% -> 0%
where the time goes in v1:
time: 623 us; the launch traced here: 618 us
  waiting for transfers between devices  292 us (47%)
  blocking collectives  122 us (20%)
  local copies, waits for them, and re-layouts  78.1 us (13%)
  matrix products  52.9 us (8%)
  starting transfers between devices  30.8 us (5%)
  other arithmetic  27.2 us (4%)
  between operations  15 us (2%)
    psum x1, waiting for transfers between devices, body(): lax.psum((local_sums[0], local_sums[1], local_sums[2], local_sums[3]), ('...  176 us
    psum x1, blocking collectives, body(): lax.psum((local_sums[0], local_sums[1], local_sums[2], local_sums[3]), ('...  76.1 us
    all_to_all x2, waiting for transfers between devices, spectral(): lax.all_to_all(rows, 'space', split_axis=3, concat_axis=2, tiled=True)  61 us
    unnamed x197, local copies, waits for them, and re-layouts  57.1 us
    psum x1, waiting for transfers between devices, body(): lax.psum(filter_terms.astype(jnp.bfloat16), 'copy').astype(jnp.float32)  55.6 us
    all_to_all x1, blocking collectives, spectral(): lax.all_to_all(jnp.stack(jnp.split(returned, lax.axis_size('space'), axis...  45.4 us
    all_to_all x2, starting transfers between devices, spectral(): lax.all_to_all(rows, 'space', split_axis=3, concat_axis=2, tiled=True)  21.8 us
    dot_general x1, matrix products, body(): preact = jnp.dot(mlp_in, weight_in, preferred_element_type=jnp.float32)  15.5 us
  transfers between devices with their start and end apart: 5, of which 4 were waited for; matrix products, arithmetic and copies ran while one was open for 14% of the time, Pallas kernels for 0%

profile of v1, /device:TPU:1, one launch (start us, length us, event | category | flops | bytes accessed | tf_op | source)
XLA Modules:
  0.0 617.8 jit_solution(5665416679440751984)
XLA Ops:
  7.2 1.6 fusion.89
  8.8 1.6 multiply_convert_fusion.8
  10.4 1.4 copy.64
  13.5 3.0 copy.66
  16.5 14.1 %all-to-all-start = ((bf16[2,1,4,256,384]{4,0,2,1,3:T(2,128)(2,1)}), bf16[2,1,4,256,384]{4,0,2,1,3:T(2,128)(2,1)}, u32[]{:S(2)}, u32[]{:S(2)}) async-start(bf16[2,1,4,256,384]{4,0,2,1,3:T(2,128)(2,1)} %copy.66), calls=%async_computation | async-start | bytes 3145728 | tf_op jit(solution)/shard_map/all_to_all | solution.py:75
  30.6 2.8 fusion.95
  34.1 1.8 copy.118
  35.9 1.0 broadcast_multiply_fusion
  36.9 1.1 multiply_convert_fusion.5
  38.0 1.0 fusion.76
  39.0 29.9 %all-to-all-done = bf16[2,1,4,256,384]{4,0,2,1,3:T(2,128)(2,1)} async-done(((bf16[2,1,4,256,384]{4,0,2,1,3:T(2,128)(2,1)}), bf16[2,1,4,256,384]{4,0,2,1,3:T(2,128)(2,1)}, u32[]{:S(2)}, u32[]{:S(2)}) %all-to-all-start) | async-done | bytes 1572896 | tf_op jit(solution)/shard_map/all_to_all | solution.py:75
  68.9 2.0 copy.67
  72.0 2.7 fusion.96
  75.7 1.0 fusion.46
  78.5 45.4 %all_to_all.40 = bf16[64,2,1,4,4,384]{5,3,1,4,2,0:T(4,128)(2,1)S(1)} all-to-all(bf16[64,2,1,4,4,384]{5,3,1,4,2,0:T(4,128)(2,1)S(1)} %constant_dynamic-update-slice_fusion), channel_id=1, replica_groups=mesh['copy'=4,'space'=64] {'space'}, dimensions={0} | all-to-all | bytes 3145728 | tf_op jit(solution)/shard_map/all_to_all | solution.py:85
  125.7 15.5 %multiply_convert_fusion = (bf16[1024,1536]{1,0:T(8,128)(2,1)}, f32[1024,1536]{1,0:T(8,128)S(1)}, f32[1024,1536]{1,0:T(8,128)S(1)}) fusion(bf16[1024,384]{1,0:T(8,128)(2,1)S(1)} %bitcast.761, bf16[384,1536]{1,0:T(8,128)(2,1)S(1)} %copy-done), kind=kOutput, calls=%fused_computation.3 | convolution fusion | flops 1310195712 | bytes 17694720 | tf_op jit(solution)/shard_map/dot_general | solution.py:102
  141.3 3.3 add_convert_fusion
  144.6 1.9 multiply_reduce_fusion.2
  146.5 1.1 multiply_reduce_fusion
  148.8 1.3 div.31
  150.1 4.0 fusion.42
  154.0 5.0 copy.79
  159.0 7.7 %all-to-all-start.2 = ((bf16[2,1,4,256,384]{4,0,2,1,3:T(2,128)(2,1)}), bf16[2,1,4,256,384]{4,0,2,1,3:T(2,128)(2,1)S(1)}, u32[]{:S(2)}, u32[]{:S(2)}) async-start(bf16[2,1,4,256,384]{4,0,2,1,3:T(2,128)(2,1)} %copy.79), calls=%async_computation.2 | async-start | bytes 3145728 | tf_op jit(solution)/shard_map/all_to_all | solution.py:75
  166.9 5.2 fusion.99
  172.1 3.2 fusion.100
  175.4 31.1 %all-to-all-done.2 = bf16[2,1,4,256,384]{4,0,2,1,3:T(2,128)(2,1)S(1)} async-done(((bf16[2,1,4,256,384]{4,0,2,1,3:T(2,128)(2,1)}), bf16[2,1,4,256,384]{4,0,2,1,3:T(2,128)(2,1)S(1)}, u32[]{:S(2)}, u32[]{:S(2)}) %all-to-all-start.2) | async-done | bytes 1572896 | tf_op jit(solution)/shard_map/all_to_all | solution.py:75
  207.7 2.5 copy.82
  210.2 4.3 fusion.97
  215.6 1.0 fusion.52
  256.0 8.6 %all-to-all-start.3 = ((bf16[64,2,1,4,4,384]{5,3,1,4,2,0:T(4,128)(2,1)}), bf16[64,2,1,4,4,384]{5,3,1,4,2,0:T(4,128)(2,1)}, u32[]{:S(2)}, u32[]{:S(2)}) async-start(bf16[64,2,1,4,4,384]{5,3,1,4,2,0:T(4,128)(2,1)} %constant_dynamic-update-slice_fusion.64), calls=%async_computation.3 | async-start | bytes 3145728 | tf_op jit(solution)/shard_map/all_to_all | solution.py:85
  264.9 3.4 fusion.59
  270.3 1.3 pad_maximum_fusion
  271.6 1.1 copy-done.14
  272.7 1.2 copy.77
  273.9 5.2 fusion.98
  279.1 1.9 copy.76
  280.9 175.6 %all-reduce.7.cloned.1.call-done = (f32[384,1536]{1,0:T(8,128)}, f32[1536,384]{1,0:T(8,128)}) async-done(((f32[384,1536]{1,0:T(8,128)}, f32[1536,384]{1,0:T(8,128)}), (f32[384,1536]{1,0:T(8,128)}, f32[1536,384]{1,0:T(8,128)})) %all-reduce.7.cloned.1.call-update) | async-done | bytes 4718608 | tf_op jit(solution)/shard_map/psum | solution.py:128
  456.6 3.0 multiply_convert_fusion.1
  459.6 1.2 multiply_convert_fusion.2
  460.8 55.6 %all-reduce.5.cloned.1.call-done = bf16[2,256,4,384]{1,3,2,0:T(8,128)(2,1)} async-done(((bf16[2,256,4,384]{1,3,2,0:T(8,128)(2,1)}), bf16[2,256,4,384]{1,3,2,0:T(8,128)(2,1)}) %all-reduce.5.cloned.1.call-update) | async-done | bytes 1572880 | tf_op jit(solution)/shard_map/psum | solution.py:124
  516.4 3.9 copy.92
  520.3 4.2 fusion.18
  524.4 76.1 %all-reduce = (f32[384]{0:T(512)}, f32[384]{0:T(512)}) all-reduce(f32[384]{0:T(512)} %get-tuple-element.28, f32[384]{0:T(512)S(1)} %copy-done.27), channel_id=1, replica_groups=mesh['copy'=4,'space'=64] {'copy','space'}, use_global_device_ids=true, to_apply=%region_12.13 | all-reduce | flops 768 | bytes 6144 | tf_op jit(solution)/shard_map/psum | solution.py:128
  600.6 1.3 broadcast_multiply_fusion.7
  601.8 1.3 broadcast_multiply_fusion.8
  603.8 3.4 fusion.17
  607.2 2.4 copy.90
  609.6 1.2 copy.91
  (217 shorter events, 53.5 us)
Async XLA Ops:
  7.2 118.5 %copy-start = (bf16[384,1536]{1,0:T(8,128)(2,1)S(1)}, bf16[384,1536]{1,0:T(8,128)(2,1)}, u32[]{:S(2)}) copy-start(bf16[384,1536]{1,0:T(8,128)(2,1)} %param.10) | copy-start | bytes 3538948
  10.4 1.8 copy-start.28
  11.9 0.9 copy-start.16
  11.9 1.0 copy-start.18
  12.8 3.7 copy-start.25
  16.5 52.4 %all-to-all-start = ((bf16[2,1,4,256,384]{4,0,2,1,3:T(2,128)(2,1)}), bf16[2,1,4,256,384]{4,0,2,1,3:T(2,128)(2,1)}, u32[]{:S(2)}, u32[]{:S(2)}) async-start(bf16[2,1,4,256,384]{4,0,2,1,3:T(2,128)(2,1)} %copy.66), calls=%async_computation | async-start | bytes 3145728 | tf_op jit(solution)/shard_map/all_to_all | solution.py:75
  34.1 40.6 %copy-start.4 = (bf16[1,256,4,384]{1,3,2,0:T(8,128)(2,1)}, bf16[1,256,4,384]{1,3,2,0:T(8,128)(2,1)S(1)}, u32[]{:S(2)}) copy-start(bf16[1,256,4,384]{1,3,2,0:T(8,128)(2,1)S(1)} %copy.116) | copy-start | bytes 2359300
  35.9 38.8 %copy-start.6 = (bf16[1,256,4,384]{1,3,2,0:T(8,128)(2,1)}, bf16[1,256,4,384]{1,3,2,0:T(8,128)(2,1)S(1)}, u32[]{:S(2)}) copy-start(bf16[1,256,4,384]{1,3,2,0:T(8,128)(2,1)S(1)} %copy.118) | copy-start | bytes 2359300
  70.9 1.0 copy-start.10
  70.9 1.0 copy-start.11
  74.7 1.0 copy-start.20
  74.7 1.0 copy-start.22
  78.4 45.4 %copy-start.17 = (bf16[1,256,256]{2,1,0:T(8,128)(2,1)S(1)}, bf16[1,256,256]{2,1,0:T(8,128)(2,1)}, u32[]{:S(2)}) copy-start(bf16[1,256,256]{2,1,0:T(8,128)(2,1)} %fusion.89) | copy-start | bytes 393220
  78.4 45.4 %copy-start.19 = (bf16[1,256,256]{2,1,0:T(8,128)(2,1)S(1)}, bf16[1,256,256]{2,1,0:T(8,128)(2,1)}, u32[]{:S(2)}) copy-start(bf16[1,256,256]{2,1,0:T(8,128)(2,1)} %multiply_convert_fusion.8) | copy-start | bytes 393220
  124.6 0.7 copy-start.24
  125.7 15.6 %copy-start.15 = (bf16[1,4,256,384]{3,2,1,0:T(8,128)(2,1)}, bf16[1,4,256,384]{3,2,1,0:T(8,128)(2,1)S(1)}, u32[]{:S(2)}) copy-start(bf16[1,4,256,384]{3,2,1,0:T(8,128)(2,1)S(1)} %multiply_convert_fusion.4) | copy-start | bytes 2359300
  125.7 15.6 %copy-start.12 = (bf16[1,4,256,384]{3,2,1,0:T(8,128)(2,1)S(1)}, bf16[1,4,256,384]{3,2,1,0:T(8,128)(2,1)}, u32[]{:S(2)}) copy-start(bf16[1,4,256,384]{3,2,1,0:T(8,128)(2,1)} %param.8) | copy-start | bytes 2359300
  125.7 15.6 %copy-start.29 = (bf16[1536,384]{1,0:T(8,128)(2,1)S(1)}, bf16[1536,384]{1,0:T(8,128)(2,1)}, u32[]{:S(2)}) copy-start(bf16[1536,384]{1,0:T(8,128)(2,1)} %param.11) | copy-start | bytes 3538948
  144.6 1.9 copy-start.30
  146.5 1.1 copy-start.3
  159.0 47.4 %all-to-all-start.2 = ((bf16[2,1,4,256,384]{4,0,2,1,3:T(2,128)(2,1)}), bf16[2,1,4,256,384]{4,0,2,1,3:T(2,128)(2,1)S(1)}, u32[]{:S(2)}, u32[]{:S(2)}) async-start(bf16[2,1,4,256,384]{4,0,2,1,3:T(2,128)(2,1)} %copy.79), calls=%async_computation.2 | async-start | bytes 3145728 | tf_op jit(solution)/shard_map/all_to_all | solution.py:75
  166.7 289.9 %all-reduce.7.cloned.1.call-start = ((), (), s32[]{:S(2)}) async-start(), calls=%async_computation.5 | async-start | bytes 9437184 | tf_op jit(solution)/shard_map/psum | solution.py:128
  166.9 5.2 copy-start.13
  166.9 5.2 copy-start.31
  210.2 4.3 copy-start.5
  210.2 4.3 copy-start.7
  214.6 1.0 copy-start.21
  214.6 1.0 copy-start.23
  256.0 264.2 %all-to-all-start.3 = ((bf16[64,2,1,4,4,384]{5,3,1,4,2,0:T(4,128)(2,1)}), bf16[64,2,1,4,4,384]{5,3,1,4,2,0:T(4,128)(2,1)}, u32[]{:S(2)}, u32[]{:S(2)}) async-start(bf16[64,2,1,4,4,384]{5,3,1,4,2,0:T(4,128)(2,1)} %constant_dynamic-update-slice_fusion.64), calls=%async_computation.3 | async-start | bytes 3145728 | tf_op jit(solution)/shard_map/all_to_all | solution.py:85
  264.6 251.8 %all-reduce.5.cloned.1.call-start = ((), (), s32[]{:S(2)}) async-start(), calls=%async_computation.4 | async-start | bytes 3145728 | tf_op jit(solution)/shard_map/psum | solution.py:124
  264.9 3.8 copy-start.1
  264.9 4.8 copy-start.2
  271.6 1.1 copy-start.14
  456.6 3.0 copy-start.9
  460.8 59.5 %copy-start.26 = (f32[4,256]{1,0:T(4,128)S(1)}, f32[4,256]{1,0:T(4,128)}, u32[]{:S(2)}) copy-start(f32[4,256]{1,0:T(4,128)} %copy-done.25) | copy-start | bytes 12292
  520.3 4.2 copy-start.27
  607.2 2.4 copy-start.8
Sparse Core Ops, SparseCore 0:
  175.5 281.0 all-reduce.6
  459.4 56.9 all-reduce.4
